TPU v7x, 32 devices: a whole 2x2x4 slice. The times are simulated.
32 devices in a mesh: grp: 2 (over y), seq: 16 (over z, x, core).
Axes of the slice: x: 2, y: 2, z: 4, core: 2. Of those that a mesh axis runs over, the one named last changes fastest.
Arguments:
- query: bfloat16 [2, 16, 1024, 128], P('grp', None, 'seq'), parts along dimension 0, may hold values from -49 to 49
- key: bfloat16 [2, 16, 1024, 128], P('grp', None, 'seq'), parts along dimension 0, may hold values from -8 to 8
- value: bfloat16 [2, 16, 1024, 128], P('grp', None, 'seq'), parts along dimension 0, may hold values from -6 to 6
- mem_key: bfloat16 [2, 16, 1024, 128], P('grp', None, 'seq'), parts along dimension 0, may hold values from -8 to 8
- mem_value: bfloat16 [2, 16, 1024, 128], P('grp', None, 'seq'), parts along dimension 0, may hold values from -6 to 6
- mem_count: int32 [2, 4], P('grp'), parts along dimension 0, may hold values from 1 to 256, as said below
- mem_factor: int32 [2, 4], P('grp'), parts along dimension 0, may hold values from 1 to 16, as said below
- out_weight: bfloat16 [2048, 3072], P('seq'), may hold values from -0.125 to 0.125
Outputs:
- block_out: bfloat16 [2, 1024, 3072], P('grp', 'seq'), parts along dimension 0
There are 2 independent parts, one for each index of `grp`. A program takes and returns all parts, laid end to end along the dimension named above; an argument that names none is the same for every part. Nothing has to cross between parts.
Inputs may be any that keep to these rules, and one draw needn't show every extreme that they name: `mem_count`: some stretch of every sequence holds exactly 256 live tokens. `mem_factor`: powers of two.
All inputs are finite; a program needn't handle non-finite values.
Results may differ from a plain program's by a relative error of at most 0.0052.
Values may be sent and summed in bfloat16 or wider, within the bound.
A program may use at most 128 MiB of HBM per device.

v0:
```python
import jax
import jax.numpy as jnp
from jax import lax
from jax.sharding import PartitionSpec as P

MCAP = 256


def per_device(query, key, value, mem_key, mem_value, mem_count, mem_factor, out_weight):
    seqs, heads, rows, width = query.shape
    slots_dev = mem_key.shape[2]
    devices = lax.axis_size("seq")
    groups = seqs * heads
    copies = devices // groups
    half = rows // copies
    feat = out_weight.shape[1]
    own_queries = (
        query.reshape(groups, half, copies, width)
        .transpose(0, 2, 1, 3)
        .reshape(groups * copies, half, width)
    )

    def spread(array, count):
        widened = jnp.broadcast_to(
            array.reshape(groups, 1, count, width), (groups, copies, count, width)
        )
        return widened.reshape(groups * copies, count, width)

    head_q, head_k, head_v, head_mk, head_mv = (
        lax.all_to_all(own_queries, "seq", split_axis=0, concat_axis=1, tiled=True),
        lax.all_to_all(spread(key, rows), "seq", split_axis=0, concat_axis=1, tiled=True),
        lax.all_to_all(spread(value, rows), "seq", split_axis=0, concat_axis=1, tiled=True),
        lax.all_to_all(spread(mem_key, slots_dev), "seq", split_axis=0, concat_axis=1, tiled=True),
        lax.all_to_all(
            spread(mem_value, slots_dev), "seq", split_axis=0, concat_axis=1, tiled=True
        ),
    )
    length_q = head_q.shape[1]
    length = head_k.shape[1]
    slots = head_mk.shape[1]
    seq_index = lax.axis_index("seq") // copies // heads
    counts = lax.dynamic_index_in_dim(mem_count, seq_index, 0, keepdims=False)
    factors = lax.dynamic_index_in_dim(mem_factor, seq_index, 0, keepdims=False)
    slot = jnp.arange(slots)
    stretch_of = slot // MCAP
    offset = slot % MCAP
    picked = stretch_of[:, None] == jnp.arange(counts.shape[0])[None, :]
    slot_count = jnp.sum(jnp.where(picked, counts[None, :], 0), 1)
    slot_factor = jnp.sum(jnp.where(picked, factors[None, :], 0), 1)
    bias = jnp.where(
        offset < slot_count, jnp.log(slot_factor.astype(jnp.float32)), jnp.float32(-1000000000.0)
    )
    full_bias = jnp.concatenate([jnp.zeros((length,), jnp.float32), bias])
    all_keys = jnp.concatenate([head_k[0], head_mk[0]], 0)
    all_vals = jnp.concatenate([head_v[0], head_mv[0]], 0)
    scale = width ** (-0.5)
    block = min(512, length_q)
    query_blocks = head_q[0].reshape(length_q // block, block, width)

    def attend(queries):
        score = (
            jnp.einsum("qd,kd->qk", queries, all_keys, preferred_element_type=jnp.float32) * scale
        )
        score = score + full_bias[None, :]
        top = jnp.max(score, axis=1, keepdims=True)
        prob = jnp.exp(score - top)
        total = jnp.sum(prob, axis=1, keepdims=True)
        weight = prob.astype(jnp.bfloat16)
        attended = jnp.dot(weight, all_vals, preferred_element_type=jnp.float32) / total
        return attended.astype(jnp.bfloat16)

    attended = lax.map(attend, query_blocks).reshape(1, length_q, width)
    returned = lax.all_to_all(attended, "seq", split_axis=1, concat_axis=0, tiled=True)
    columns = returned.reshape(seqs, heads, copies, half, width).transpose(0, 3, 2, 1, 4)
    columns = columns.reshape(seqs * rows, heads * width)
    mixed = jnp.dot(
        columns,
        lax.all_gather(out_weight, "seq", axis=0, tiled=True),
        preferred_element_type=jnp.float32,
    )
    result = mixed.reshape(seqs, rows, feat).astype(jnp.bfloat16)
    return result


def solution(mesh):
    in_specs = (
        P("grp", None, "seq", None),
        P("grp", None, "seq", None),
        P("grp", None, "seq", None),
        P("grp", None, "seq", None),
        P("grp", None, "seq", None),
        P("grp", None),
        P("grp", None),
        P("seq", None),
    )
    out_specs = P("grp", "seq", None)
    return jax.shard_map(
        per_device, mesh=mesh, in_specs=in_specs, out_specs=out_specs, check_vma=False
    )
```

profile of v0, /device:TPU:0, one launch (start us, length us, event | category | flops | bytes accessed | tf_op | source)
XLA Modules:
  0.0 152.8 jit_solution(13897523027870306095)
XLA Ops:
  6.5 0.0 all-gather.2.cloned.1.call-start
  6.5 0.7 all-gather.2.cloned.1.call-update
  7.3 17.4 %all_to_all.24 = bf16[16,64,128]{2,1,0:T(8,128)(2,1)S(1)} all-to-all(bf16[16,64,128]{2,1,0:T(8,128)(2,1)} %bitcast.58), channel_id=1, replica_groups=mesh['grp'=2,'seq'=16] {'seq'}, dimensions={0} | all-to-all | bytes 524288 | tf_op jit(solution)/shard_map/all_to_all | solution.py:31
  24.7 18.1 %all_to_all.25 = bf16[16,64,128]{2,1,0:T(8,128)(2,1)S(1)} all-to-all(bf16[16,64,128]{2,1,0:T(8,128)(2,1)} %bitcast.59), channel_id=1, replica_groups=mesh['grp'=2,'seq'=16] {'seq'}, dimensions={0} | all-to-all | bytes 524288 | tf_op jit(solution)/shard_map/all_to_all | solution.py:33
  42.8 17.7 %all_to_all.26 = bf16[16,64,128]{2,1,0:T(8,128)(2,1)S(1)} all-to-all(bf16[16,64,128]{2,1,0:T(8,128)(2,1)} %bitcast.60), channel_id=1, replica_groups=mesh['grp'=2,'seq'=16] {'seq'}, dimensions={0} | all-to-all | bytes 524288 | tf_op jit(solution)/shard_map/all_to_all | solution.py:32
  60.5 4.0 %all-to-all-start.4 = ((bf16[16,64,128]{2,1,0:T(8,128)(2,1)}), bf16[16,64,128]{2,1,0:T(8,128)(2,1)S(1)}, u32[]{:S(2)}, u32[]{:S(2)}) async-start(bf16[16,64,128]{2,1,0:T(8,128)(2,1)} %bitcast.61), calls=%async_computation.4 | async-start | bytes 524288 | tf_op jit(solution)/shard_map/all_to_all | solution.py:34
  64.5 0.8 select_reduce_fusion.1
  65.3 13.5 %all-to-all-done.4 = bf16[16,64,128]{2,1,0:T(8,128)(2,1)S(1)} async-done(((bf16[16,64,128]{2,1,0:T(8,128)(2,1)}), bf16[16,64,128]{2,1,0:T(8,128)(2,1)S(1)}, u32[]{:S(2)}, u32[]{:S(2)}) %all-to-all-start.4) | async-done | bytes 262176 | tf_op jit(solution)/shard_map/all_to_all | solution.py:34
  78.8 5.9 %all-to-all-start = ((bf16[16,64,128]{2,1,0:T(8,128)(2,1)}), bf16[16,64,128]{2,1,0:T(8,128)(2,1)S(1)}, u32[]{:S(2)}, u32[]{:S(2)}) async-start(bf16[16,64,128]{2,1,0:T(8,128)(2,1)} %bitcast.62), calls=%async_computation | async-start | bytes 524288 | tf_op jit(solution)/shard_map/all_to_all | solution.py:30
  84.8 14.5 %all-to-all-done = bf16[16,64,128]{2,1,0:T(8,128)(2,1)S(1)} async-done(((bf16[16,64,128]{2,1,0:T(8,128)(2,1)}), bf16[16,64,128]{2,1,0:T(8,128)(2,1)S(1)}, u32[]{:S(2)}, u32[]{:S(2)}) %all-to-all-start) | async-done | bytes 262176 | tf_op jit(solution)/shard_map/all_to_all | solution.py:30
  99.3 5.6 %while.10 = (s32[]{:T(128)}, bf16[2,512,128]{2,1,0:T(8,128)(2,1)S(1)}, bf16[2,512,128]{2,1,0:T(8,128)(2,1)S(1)}, bf16[2048,128]{1,0:T(8,128)(2,1)S(1)}, f32[2048...) while((s32[]{:T(128)}, bf16[2,512,128]{2,1,0:T(8,128)(2,1)S(1)}, ...), condition=%wide.region_5.6_spmd, body=%wide.region_2.5_spmd.sunk | while | flops 548535296 | bytes 13928533 | solution.py:72
  99.3 0.8 fusion.43
  100.1 1.0 fusion.44
  101.0 1.0 fusion.45
  102.1 0.8 fusion.43
  102.9 1.0 fusion.44
  103.8 1.0 fusion.45
  104.9 0.4 copy.22
  105.3 0.5 broadcast.60
  105.8 2.2 %reduce = bf16[1024,128]{1,0:T(8,128)(2,1)S(1)} reduce(bf16[1024,1,128]{2,1,0:T(2,128)(2,1)S(1)} %bitcast.50, bf16[]{:T(256)} %broadcast.60), dimensions={1}, to_apply=%bitcast.39.reduce_sub_computation | reduce | bytes 524290
  108.0 0.1 reshape.54
  108.1 20.1 %all_to_all.27 = bf16[16,2,4096]{2,1,0:T(2,128)(2,1)S(1)} all-to-all(bf16[16,2,4096]{2,1,0:T(2,128)(2,1)S(1)} %reshape.54), channel_id=1, replica_groups=mesh['grp'=2,'seq'=16] {'seq'}, dimensions={0} | all-to-all | bytes 524288 | tf_op jit(solution)/shard_map/all_to_all | solution.py:73
  128.2 0.3 reshape.55
  128.5 0.2 copy.14
  128.7 9.6 %all-gather.2.cloned.1.call-done = bf16[2048,3072]{1,0:T(8,128)(2,1)} async-done(((bf16[128,3072]{1,0:T(8,128)(2,1)}), bf16[2048,3072]{1,0:T(8,128)(2,1)}) %all-gather.2.cloned.1.call-update) | async-done | bytes 12582928 | tf_op jit(solution)/shard_map/all_gather | solution.py:78
  138.3 7.6 %fusion.22 = bf16[1,64,3072]{2,1,0:T(8,128)(2,1)} fusion(bf16[2048,3072]{1,0:T(8,128)(2,1)} %all-gather.2.cloned.1.call-done, bf16[8,8,16,128]{3,2,1,0:T(8,128)(2,1)S(1)} %bitcast.51), kind=kOutput, calls=%fused_computation.16 | convolution fusion | flops 805502976 | bytes 13238272 | tf_op jit(solution)/shard_map/dot_general | solution.py:76
  (7 shorter events, 0.1 us)
Async XLA Ops:
  6.5 131.8 %all-gather.2.cloned.1.call-start = ((), (), s32[]{:S(2)}) async-start(), calls=%async_computation.6 | async-start | bytes 13369344 | tf_op jit(solution)/shard_map/all_gather | solution.py:78
  60.5 18.3 %all-to-all-start.4 = ((bf16[16,64,128]{2,1,0:T(8,128)(2,1)}), bf16[16,64,128]{2,1,0:T(8,128)(2,1)S(1)}, u32[]{:S(2)}, u32[]{:S(2)}) async-start(bf16[16,64,128]{2,1,0:T(8,128)(2,1)} %bitcast.61), calls=%async_computation.4 | async-start | bytes 524288 | tf_op jit(solution)/shard_map/all_to_all | solution.py:34
  78.8 20.5 %all-to-all-start = ((bf16[16,64,128]{2,1,0:T(8,128)(2,1)}), bf16[16,64,128]{2,1,0:T(8,128)(2,1)S(1)}, u32[]{:S(2)}, u32[]{:S(2)}) async-start(bf16[16,64,128]{2,1,0:T(8,128)(2,1)} %bitcast.62), calls=%async_computation | async-start | bytes 524288 | tf_op jit(solution)/shard_map/all_to_all | solution.py:30
Sparse Core Ops, SparseCore 0:
  9.6 128.6 all-gather.1
where the time goes:
time: 154 us; the launch traced here: 153 us
  blocking collectives  73.4 us (48%)
  waiting for transfers between devices  38.3 us (25%)
  between operations  13.5 us (9%)
  matrix products  11.3 us (7%)
  starting transfers between devices  9.82 us (6%)
  other arithmetic  4.96 us (3%)
    all_to_all x1, blocking collectives, per_device(): lax.all_to_all(attended, 'seq', split_axis=1, concat_axis=0, tiled=True)  20.1 us
    all_to_all x1, blocking collectives, per_device(): lax.all_to_all(spread(mem_key, slots_dev), 'seq', split_axis=0, concat_ax...  18.1 us
    all_to_all x1, blocking collectives, per_device(): lax.all_to_all(spread(value, rows), 'seq', split_axis=0, concat_axis=1, t...  17.7 us
    all_to_all x1, blocking collectives, per_device(): lax.all_to_all(spread(key, rows), 'seq', split_axis=0, concat_axis=1, til...  17.4 us
    all_to_all x1, waiting for transfers between devices, per_device(): lax.all_to_all(own_queries, 'seq', split_axis=0, concat_axis=1, tiled=True)  14.5 us
    all_to_all x1, waiting for transfers between devices, per_device(): lax.all_to_all(spread(mem_value, slots_dev), 'seq', split_axis=0, concat_...  13.5 us
    all_gather x1, waiting for transfers between devices, per_device(): lax.all_gather(out_weight, 'seq', axis=0, tiled=True)  9.63 us
    dot_general x1, matrix products, per_device(): jnp.dot(columns, lax.all_gather(out_weight, 'seq', axis=0, tiled=True), p...  7.62 us
  transfers between devices with their start and end apart: 3, of which 3 were waited for; matrix products, arithmetic and copies ran while one was open for 7% of the time, Pallas kernels for 0%

commit v1 on v0

--- a/solution.py
+++ b/solution.py
@@ -4,6 +4,12 @@
 from jax.sharding import PartitionSpec as P
 
 MCAP = 256
+
+
+def stacked_exchange(array, mesh_axis, split, join):
+    pieces = jnp.split(array, lax.axis_size(mesh_axis), axis=split)
+    incoming = lax.all_to_all(jnp.stack(pieces), mesh_axis, 0, 0)
+    return jnp.concatenate(incoming, axis=join)
 
 
 def per_device(query, key, value, mem_key, mem_value, mem_count, mem_factor, out_weight):
@@ -31,9 +37,7 @@
         lax.all_to_all(spread(key, rows), "seq", split_axis=0, concat_axis=1, tiled=True),
         lax.all_to_all(spread(value, rows), "seq", split_axis=0, concat_axis=1, tiled=True),
         lax.all_to_all(spread(mem_key, slots_dev), "seq", split_axis=0, concat_axis=1, tiled=True),
-        lax.all_to_all(
-            spread(mem_value, slots_dev), "seq", split_axis=0, concat_axis=1, tiled=True
-        ),
+        stacked_exchange(spread(mem_value, slots_dev), "seq", 0, 1),
     )
     length_q = head_q.shape[1]
     length = head_k.shape[1]

time: 154 us -> 160 us (1.039)
  local copies, waits for them, and re-layouts: 1.47 us -> 13 us
  waiting for transfers between devices: 38.3 us -> 29.1 us
  starting transfers between devices: 9.82 us -> 11.5 us
    unnamed x4 -> x19, local copies, waits for them, and re-layouts: 0.88 us -> 11.7 us
    all_gather x1, waiting for transfers between devices: 9.63 us -> 0.02 us  [per_device(): lax.all_gather(out_weight, 'seq', axis=0, tiled=True)]
    all_to_all x1, blocking collectives: 20.1 us -> 15.6 us  [per_device(): lax.all_to_all(attended, 'seq', split_axis=1, concat_axis=0, tiled=True)]
    all_to_all x1, blocking collectives: 18.1 us -> 21.8 us  [stacked_exchange(): incoming = lax.all_to_all(jnp.stack(pieces), mesh_axis, 0, 0)]
    all_to_all x1, starting transfers between devices: 3.95 us -> 5.86 us  [per_device(): lax.all_to_all(spread(mem_key, slots_dev), 'seq', split_axis=0, concat_ax...]
    all_to_all x1, blocking collectives: 17.7 us -> 19.6 us  [per_device(): lax.all_to_all(spread(value, rows), 'seq', split_axis=0, concat_axis=1, t...]
  transfers between devices with their start and end apart: 3 -> 3, of which waited for: 3 -> 2; matrix products, arithmetic and copies ran while one was open for 7% -> 14% of each run, Pallas kernels for 0% -> 0%
where the time goes in v1:
time: 160 us; the launch traced here: 158 us
  blocking collectives  74.4 us (47%)
  waiting for transfers between devices  29.1 us (18%)
  between operations  13.5 us (8%)
  local copies, waits for them, and re-layouts  13 us (8%)
  starting transfers between devices  11.5 us (7%)
  matrix products  11.3 us (7%)
  other arithmetic  4.96 us (3%)
    all_to_all x1, blocking collectives, stacked_exchange(): incoming = lax.all_to_all(jnp.stack(pieces), mesh_axis, 0, 0)  21.8 us
    all_to_all x1, blocking collectives, per_device(): lax.all_to_all(spread(value, rows), 'seq', split_axis=0, concat_axis=1, t...  19.6 us
    all_to_all x1, blocking collectives, per_device(): lax.all_to_all(spread(key, rows), 'seq', split_axis=0, concat_axis=1, til...  17.5 us
    all_to_all x1, blocking collectives, per_device(): lax.all_to_all(attended, 'seq', split_axis=1, concat_axis=0, tiled=True)  15.6 us
    all_to_all x1, waiting for transfers between devices, per_device(): lax.all_to_all(own_queries, 'seq', split_axis=0, concat_axis=1, tiled=True)  14.5 us
    all_to_all x1, waiting for transfers between devices, per_device(): lax.all_to_all(spread(mem_key, slots_dev), 'seq', split_axis=0, concat_ax...  13.8 us
    unnamed x19, local copies, waits for them, and re-layouts  11.7 us
    dot_general x1, matrix products, per_device(): jnp.dot(columns, lax.all_gather(out_weight, 'seq', axis=0, tiled=True), p...  7.62 us
  transfers between devices with their start and end apart: 3, of which 2 were waited for; matrix products, arithmetic and copies ran while one was open for 14% of the time, Pallas kernels for 0%

profile of v1, /device:TPU:0, one launch (start us, length us, event | category | flops | bytes accessed | tf_op | source)
XLA Modules:
  0.0 157.8 jit_solution(8750959512103569811)
XLA Ops:
  6.5 0.0 all-gather.2.cloned.1.call-start
  6.5 0.7 all-gather.2.cloned.1.call-update
  7.3 0.7 constant_dynamic-update-slice_fusion.15
  8.0 0.7 constant_dynamic-update-slice_fusion.14
  8.7 0.7 constant_dynamic-update-slice_fusion.13
  9.4 0.7 constant_dynamic-update-slice_fusion.12
  10.2 0.7 constant_dynamic-update-slice_fusion.11
  10.9 0.7 constant_dynamic-update-slice_fusion.10
  11.6 0.7 constant_dynamic-update-slice_fusion.9
  12.3 0.7 constant_dynamic-update-slice_fusion.8
  13.1 0.7 constant_dynamic-update-slice_fusion.7
  13.8 0.7 constant_dynamic-update-slice_fusion.6
  14.5 0.7 constant_dynamic-update-slice_fusion.5
  15.2 0.7 constant_dynamic-update-slice_fusion.4
  15.9 0.7 constant_dynamic-update-slice_fusion.3
  16.7 0.7 constant_dynamic-update-slice_fusion.2
  17.4 0.7 constant_dynamic-update-slice_fusion.1
  18.1 0.7 constant_dynamic-update-slice_fusion
  18.8 21.8 %all_to_all.24 = bf16[16,1,64,128]{3,2,1,0:T(8,128)(2,1)S(1)} all-to-all(bf16[16,1,64,128]{3,2,1,0:T(8,128)(2,1)S(1)} %constant_dynamic-update-slice_fusion), channel_id=1, replica_groups=mesh['grp'=2,'seq'=16] {'seq'}, dimensions={0} | all-to-all | bytes 524288 | tf_op jit(solution)/shard_map/all_to_all | solution.py:11
  40.6 19.6 %all_to_all.25 = bf16[16,64,128]{2,1,0:T(8,128)(2,1)S(1)} all-to-all(bf16[16,64,128]{2,1,0:T(8,128)(2,1)} %bitcast.57), channel_id=1, replica_groups=mesh['grp'=2,'seq'=16] {'seq'}, dimensions={0} | all-to-all | bytes 524288 | tf_op jit(solution)/shard_map/all_to_all | solution.py:38
  60.3 17.5 %all_to_all.52 = bf16[16,64,128]{2,1,0:T(8,128)(2,1)S(1)} all-to-all(bf16[16,64,128]{2,1,0:T(8,128)(2,1)} %bitcast.58), channel_id=1, replica_groups=mesh['grp'=2,'seq'=16] {'seq'}, dimensions={0} | all-to-all | bytes 524288 | tf_op jit(solution)/shard_map/all_to_all | solution.py:37
  77.7 5.9 %all-to-all-start.2 = ((bf16[16,64,128]{2,1,0:T(8,128)(2,1)}), bf16[16,64,128]{2,1,0:T(8,128)(2,1)S(1)}, u32[]{:S(2)}, u32[]{:S(2)}) async-start(bf16[16,64,128]{2,1,0:T(8,128)(2,1)} %bitcast.59), calls=%async_computation.2 | async-start | bytes 524288 | tf_op jit(solution)/shard_map/all_to_all | solution.py:39
  83.6 0.8 select_reduce_fusion.1
  84.4 13.8 %all-to-all-done.2 = bf16[16,64,128]{2,1,0:T(8,128)(2,1)S(1)} async-done(((bf16[16,64,128]{2,1,0:T(8,128)(2,1)}), bf16[16,64,128]{2,1,0:T(8,128)(2,1)S(1)}, u32[]{:S(2)}, u32[]{:S(2)}) %all-to-all-start.2) | async-done | bytes 262176 | tf_op jit(solution)/shard_map/all_to_all | solution.py:39
  98.2 5.6 %all-to-all-start = ((bf16[16,64,128]{2,1,0:T(8,128)(2,1)}), bf16[16,64,128]{2,1,0:T(8,128)(2,1)S(1)}, u32[]{:S(2)}, u32[]{:S(2)}) async-start(bf16[16,64,128]{2,1,0:T(8,128)(2,1)} %bitcast.60), calls=%async_computation | async-start | bytes 524288 | tf_op jit(solution)/shard_map/all_to_all | solution.py:36
  104.0 14.5 %all-to-all-done = bf16[16,64,128]{2,1,0:T(8,128)(2,1)S(1)} async-done(((bf16[16,64,128]{2,1,0:T(8,128)(2,1)}), bf16[16,64,128]{2,1,0:T(8,128)(2,1)S(1)}, u32[]{:S(2)}, u32[]{:S(2)}) %all-to-all-start) | async-done | bytes 262176 | tf_op jit(solution)/shard_map/all_to_all | solution.py:36
  118.5 5.6 %while.10 = (s32[]{:T(128)}, bf16[2,512,128]{2,1,0:T(8,128)(2,1)S(1)}, bf16[2,512,128]{2,1,0:T(8,128)(2,1)S(1)}, bf16[2048,128]{1,0:T(8,128)(2,1)S(1)}, f32[2048...) while((s32[]{:T(128)}, bf16[2,512,128]{2,1,0:T(8,128)(2,1)S(1)}, ...), condition=%wide.region_5.6_spmd, body=%wide.region_2.5_spmd.sunk | while | flops 548535296 | bytes 13928533 | solution.py:76
  118.5 0.8 fusion.43
  119.3 1.0 fusion.44
  120.2 1.0 fusion.45
  121.3 0.8 fusion.43
  122.1 1.0 fusion.44
  123.0 1.0 fusion.45
  124.1 0.4 copy.22
  124.5 0.5 broadcast.60
  125.0 2.2 %reduce = bf16[1024,128]{1,0:T(8,128)(2,1)S(1)} reduce(bf16[1024,1,128]{2,1,0:T(2,128)(2,1)S(1)} %bitcast.49, bf16[]{:T(256)} %broadcast.60), dimensions={1}, to_apply=%bitcast.38.reduce_sub_computation | reduce | bytes 524290
  127.2 0.1 reshape.82
  127.3 15.6 %all_to_all.53 = bf16[16,2,4096]{2,1,0:T(2,128)(2,1)S(1)} all-to-all(bf16[16,2,4096]{2,1,0:T(2,128)(2,1)S(1)} %reshape.82), channel_id=1, replica_groups=mesh['grp'=2,'seq'=16] {'seq'}, dimensions={0} | all-to-all | bytes 524288 | tf_op jit(solution)/shard_map/all_to_all | solution.py:77
  142.8 0.3 reshape.83
  143.2 0.2 copy.14
  143.3 0.0 all-gather.2.cloned.1.call-done
  143.4 7.6 %fusion.22 = bf16[1,64,3072]{2,1,0:T(8,128)(2,1)} fusion(bf16[2048,3072]{1,0:T(8,128)(2,1)} %all-gather.2.cloned.1.call-done, bf16[8,8,16,128]{3,2,1,0:T(8,128)(2,1)S(1)} %bitcast.50), kind=kOutput, calls=%fused_computation.16 | convolution fusion | flops 805502976 | bytes 13238272 | tf_op jit(solution)/shard_map/dot_general | solution.py:80
  (7 shorter events, 0.1 us)
Async XLA Ops:
  6.5 136.8 %all-gather.2.cloned.1.call-start = ((), (), s32[]{:S(2)}) async-start(), calls=%async_computation.6 | async-start | bytes 13369344 | tf_op jit(solution)/shard_map/all_gather | solution.py:82
  77.7 20.5 %all-to-all-start.2 = ((bf16[16,64,128]{2,1,0:T(8,128)(2,1)}), bf16[16,64,128]{2,1,0:T(8,128)(2,1)S(1)}, u32[]{:S(2)}, u32[]{:S(2)}) async-start(bf16[16,64,128]{2,1,0:T(8,128)(2,1)} %bitcast.59), calls=%async_computation.2 | async-start | bytes 524288 | tf_op jit(solution)/shard_map/all_to_all | solution.py:39
  98.2 20.3 %all-to-all-start = ((bf16[16,64,128]{2,1,0:T(8,128)(2,1)}), bf16[16,64,128]{2,1,0:T(8,128)(2,1)S(1)}, u32[]{:S(2)}, u32[]{:S(2)}) async-start(bf16[16,64,128]{2,1,0:T(8,128)(2,1)} %bitcast.60), calls=%async_computation | async-start | bytes 524288 | tf_op jit(solution)/shard_map/all_to_all | solution.py:36
Sparse Core Ops, SparseCore 0:
  9.6 128.0 all-gather.1
